TPU v7x, 32 devices: a whole 2x2x4 slice. The times are simulated.
32 devices in a mesh: fsdp: 8 (over z, y), tp: 4 (over x, core).
Axes of the slice: x: 2, y: 2, z: 4, core: 2. Of those that a mesh axis runs over, the one named last changes fastest.
Arguments:
- layer_input: bfloat16 [8192, 768], P(('fsdp', 'tp')), may hold values from -12 to 12
- out_cotangent: bfloat16 [8192, 768], P(('fsdp', 'tp')), may hold values from -12 to 12
- segments: int32 [8, 1024], P('fsdp'), may hold values from 0 to 3, never falling along the last dimension, each value on 1 to 512 neighbouring positions
- norm_gain: float32 [768], replicated, may hold values from 0.5 to 1.5
- norm_bias: float32 [768], replicated, may hold values from -3 to 3
- qkv_weight: bfloat16 [768, 2304], P('fsdp', 'tp'), may hold values from -20 to 20
- qkv_bias: float32 [2304], P('tp'), may hold values from -3 to 3
- out_weight: bfloat16 [768, 768], P('tp', 'fsdp'), may hold values from -0.875 to 0.875
- out_bias: float32 [768], replicated, may hold values from -3 to 3
- up_weight: bfloat16 [768, 3072], P('fsdp', 'tp'), may hold values from -0.21875 to 0.21875
- up_bias: float32 [3072], P('tp'), may hold values from -3 to 3
- down_weight: bfloat16 [3072, 768], P('tp', 'fsdp'), may hold values from -0.109375 to 0.109375
- down_bias: float32 [768], replicated, may hold values from -3 to 3
Outputs:
- layer_output: bfloat16 [8192, 768], P(('fsdp', 'tp'))
- input_grad: bfloat16 [8192, 768], P(('fsdp', 'tp'))
- norm_gain_grad: float32 [768], replicated
- norm_bias_grad: float32 [768], replicated
- qkv_weight_grad: float32 [768, 2304], P('fsdp', 'tp')
- qkv_bias_grad: float32 [2304], P('tp')
- out_weight_grad: float32 [768, 768], P('tp', 'fsdp')
- out_bias_grad: float32 [768], replicated
- up_weight_grad: float32 [768, 3072], P('fsdp', 'tp')
- up_bias_grad: float32 [3072], P('tp')
- down_weight_grad: float32 [3072, 768], P('tp', 'fsdp')
- down_bias_grad: float32 [768], replicated
Inputs may be any that keep to these rules, and one draw needn't show every extreme that they name: `segments`: each row is one sequence of 1024 tokens; its numbers name documents, never fall along the row, and each document spans 1 to 512 tokens, one exactly 512.
All inputs are finite; a program needn't handle non-finite values.
Results may differ from a plain program's by a relative error of at most 0.01.
Values may be sent and summed in bfloat16 or wider, within the bound.
A program may use at most 128 MiB of HBM per device.

v0:
```python
import jax
import jax.numpy as jnp
from jax import lax
from jax.sharding import PartitionSpec as P

HEAD_DIM = 64
ROT = 16
EPSILON = 1e-05
ROTARY_BASE = 10000.0


def layer_norm(values, gain, shift):
    center = values - jnp.mean(values, axis=-1, keepdims=True)
    spread = jnp.mean(center * center, axis=-1, keepdims=True)
    inverse = lax.rsqrt(spread + EPSILON)
    normed = center * inverse
    return (normed, inverse, normed * gain + shift)


def gelu_value(pre_act):
    return 0.5 * pre_act * (1.0 + lax.erf(pre_act * 0.7071067811865476))


def gelu_slope(pre_act):
    return (
        0.5 * (1.0 + lax.erf(pre_act * 0.7071067811865476))
        + pre_act * jnp.exp(-0.5 * pre_act * pre_act) * 0.3989422804014327
    )


def positions_of(segment_row):
    length = segment_row.shape[0]
    counter = jnp.arange(length, dtype=jnp.int32)
    is_start = jnp.concatenate(
        [jnp.ones((1,), dtype=jnp.bool_), segment_row[1:] != segment_row[:-1]]
    )
    starts = lax.cummax(jnp.where(is_start, counter, jnp.zeros_like(counter)), axis=0)
    return counter - starts


def rotary_tables(positions):
    halves = ROT // 2
    inverse_freq = ROTARY_BASE ** (-(jnp.arange(halves, dtype=jnp.float32) * 2.0) / ROT)
    angles = positions.astype(jnp.float32)[:, None] * inverse_freq[None, :]
    cos_table = jnp.cos(angles)
    sin_table = jnp.sin(angles)
    return (
        jnp.concatenate([cos_table, cos_table], axis=-1),
        jnp.concatenate([sin_table, sin_table], axis=-1),
    )


def rotate(tensor, cos_table, sin_table):
    halves = ROT // 2
    turned_part = tensor[..., :ROT]
    turned = jnp.concatenate([-turned_part[..., halves:], turned_part[..., :halves]], axis=-1)
    spun = turned_part * cos_table[:, None, :] + turned * sin_table[:, None, :]
    return jnp.concatenate([spun, tensor[..., ROT:]], axis=-1)


def unrotate(grad_in, cos_table, sin_table):
    halves = ROT // 2
    turned_part = grad_in[..., :ROT]
    scaled = turned_part * sin_table[:, None, :]
    back = jnp.concatenate([scaled[..., halves:], -scaled[..., :halves]], axis=-1)
    return jnp.concatenate(
        [turned_part * cos_table[:, None, :] + back, grad_in[..., ROT:]], axis=-1
    )


def cross_rows(left, right):
    return lax.dot_general(
        left, right, (((0,), (0,)), ((), ())), preferred_element_type=jnp.float32
    )


def cross_cols(left, right):
    return lax.dot_general(
        left, right, (((1,), (1,)), ((), ())), preferred_element_type=jnp.float32
    )


def block_scores(queries, keys_in, segment_row, first_row, last_row, score_scale):
    counter = jnp.arange(last_row, dtype=jnp.int32)
    allowed = (segment_row[first_row:last_row, None] == segment_row[None, :last_row]) & (
        counter[first_row:last_row, None] >= counter[None, :last_row]
    )
    scores = cross_cols(queries[first_row:last_row], keys_in[:last_row]) * score_scale
    return jnp.where(allowed, scores, -jnp.inf)


def head_forward(queries, keys_in, values_in, segment_row, score_scale):
    length = queries.shape[0]
    span = min(512, length)
    mixed_parts = []
    total_parts = []
    for first_row in range(0, length, span):
        last_row = min(first_row + span, length)
        scores = block_scores(queries, keys_in, segment_row, first_row, last_row, score_scale)
        highest = jnp.max(scores, axis=-1, keepdims=True)
        log_total = highest + jnp.log(jnp.sum(jnp.exp(scores - highest), axis=-1, keepdims=True))
        weights = jnp.exp(scores - log_total).astype(jnp.bfloat16)
        mixed_parts.append(
            jnp.dot(weights, values_in[:last_row], preferred_element_type=jnp.float32).astype(
                jnp.bfloat16
            )
        )
        total_parts.append(log_total)
    return (jnp.concatenate(mixed_parts, axis=0), jnp.concatenate(total_parts, axis=0))


def head_backward(
    queries, keys_in, values_in, mixed, grad_mixed, log_total, segment_row, score_scale
):
    length = queries.shape[0]
    span = min(512, length)
    delta = jnp.sum(
        grad_mixed.astype(jnp.float32) * mixed.astype(jnp.float32), axis=-1, keepdims=True
    )
    grad_keys = jnp.zeros(keys_in.shape, jnp.float32)
    grad_values = jnp.zeros(values_in.shape, jnp.float32)
    query_parts = []
    for first_row in range(0, length, span):
        last_row = min(first_row + span, length)
        padding = ((0, length - last_row), (0, 0))
        scores = block_scores(queries, keys_in, segment_row, first_row, last_row, score_scale)
        probs = jnp.exp(scores - log_total[first_row:last_row])
        weights = probs.astype(jnp.bfloat16)
        grad_rows = grad_mixed[first_row:last_row]
        grad_values = grad_values + jnp.pad(cross_rows(weights, grad_rows), padding)
        grad_probs = cross_cols(grad_rows, values_in[:last_row])
        grad_scores = (probs * (grad_probs - delta[first_row:last_row]) * score_scale).astype(
            jnp.bfloat16
        )
        query_parts.append(
            jnp.dot(grad_scores, keys_in[:last_row], preferred_element_type=jnp.float32)
        )
        grad_keys = grad_keys + jnp.pad(
            cross_rows(grad_scores, queries[first_row:last_row]), padding
        )
    return (jnp.concatenate(query_parts, axis=0), grad_keys, grad_values)


def body(
    layer_input,
    out_cotangent,
    segments,
    norm_gain,
    norm_bias,
    qkv_weight,
    qkv_bias,
    out_weight,
    out_bias,
    up_weight,
    up_bias,
    down_weight,
    down_bias,
):
    score_scale = HEAD_DIM ** (-0.5)
    own_rows = layer_input.astype(jnp.float32)
    normed, inverse, shifted = layer_norm(own_rows, norm_gain, norm_bias)
    features = lax.all_gather(shifted.astype(jnp.bfloat16), "tp", axis=0, tiled=True)
    length = features.shape[0]
    full_qkv, full_out, full_up, full_down = (
        lax.all_gather(qkv_weight, "fsdp", axis=0, tiled=True),
        lax.all_gather(out_weight, "fsdp", axis=1, tiled=True),
        lax.all_gather(up_weight, "fsdp", axis=0, tiled=True),
        lax.all_gather(down_weight, "fsdp", axis=1, tiled=True),
    )
    local_heads = full_qkv.shape[1] // (3 * HEAD_DIM)
    segment_row = segments[0]
    cos_table, sin_table = rotary_tables(positions_of(segment_row))
    packed = (jnp.dot(features, full_qkv, preferred_element_type=jnp.float32) + qkv_bias).reshape(
        length, local_heads, 3, HEAD_DIM
    )
    queries = rotate(packed[:, :, 0], cos_table, sin_table).astype(jnp.bfloat16).transpose(1, 0, 2)
    keys_all = rotate(packed[:, :, 1], cos_table, sin_table).astype(jnp.bfloat16).transpose(1, 0, 2)
    values_all = packed[:, :, 2].astype(jnp.bfloat16).transpose(1, 0, 2)

    def forward_head(member):
        return head_forward(member[0], member[1], member[2], segment_row, score_scale)

    mixed, log_total = lax.map(forward_head, (queries, keys_all, values_all))
    mixed_rows = mixed.transpose(1, 0, 2).reshape(length, local_heads * HEAD_DIM)
    pre_act = jnp.dot(features, full_up, preferred_element_type=jnp.float32) + up_bias
    gelu_rows = gelu_value(pre_act).astype(jnp.bfloat16)
    partial_value = jnp.dot(mixed_rows, full_out, preferred_element_type=jnp.float32) + jnp.dot(
        gelu_rows, full_down, preferred_element_type=jnp.float32
    )
    branch = lax.psum_scatter(partial_value, "tp", scatter_dimension=0, tiled=True)
    layer_output = (own_rows + branch + out_bias + down_bias).astype(jnp.bfloat16)
    grad_rows = lax.all_gather(out_cotangent, "tp", axis=0, tiled=True)
    back_qkv, back_out, back_up, back_down = (full_qkv, full_out, full_up, full_down)
    down_grad = cross_rows(gelu_rows, grad_rows)
    grad_pre = cross_cols(grad_rows, back_down) * gelu_slope(pre_act)
    pre_grads = grad_pre.astype(jnp.bfloat16)
    up_grad = cross_rows(features, pre_grads)
    up_bias_part = jnp.sum(grad_pre, axis=0)
    feature_grad = cross_cols(pre_grads, back_up)
    out_grad = cross_rows(mixed_rows, grad_rows)
    mixed_grad = (
        cross_cols(grad_rows, back_out)
        .astype(jnp.bfloat16)
        .reshape(length, local_heads, HEAD_DIM)
        .transpose(1, 0, 2)
    )

    def backward_head(member):
        return head_backward(
            member[0],
            member[1],
            member[2],
            member[3],
            member[4],
            member[5],
            segment_row,
            score_scale,
        )

    grad_q, grad_k, grad_v = lax.map(
        backward_head, (queries, keys_all, values_all, mixed, mixed_grad, log_total)
    )
    grad_q = unrotate(grad_q.transpose(1, 0, 2), cos_table, sin_table)
    grad_k = unrotate(grad_k.transpose(1, 0, 2), cos_table, sin_table)
    grad_v = grad_v.transpose(1, 0, 2)
    packed_grad = jnp.stack([grad_q, grad_k, grad_v], axis=2).reshape(
        length, 3 * local_heads * HEAD_DIM
    )
    qkv_bias_part = jnp.sum(packed_grad, axis=0)
    packed_bf = packed_grad.astype(jnp.bfloat16)
    qkv_grad = cross_rows(features, packed_bf)
    feature_grad = feature_grad + cross_cols(packed_bf, back_qkv)
    qkv_grad, out_grad, up_grad, down_grad = (
        lax.psum_scatter(qkv_grad, "fsdp", scatter_dimension=0, tiled=True),
        lax.psum_scatter(out_grad, "fsdp", scatter_dimension=1, tiled=True),
        lax.psum_scatter(up_grad, "fsdp", scatter_dimension=0, tiled=True),
        lax.psum_scatter(down_grad, "fsdp", scatter_dimension=1, tiled=True),
    )
    row_grad = lax.psum_scatter(feature_grad, "tp", scatter_dimension=0, tiled=True)
    cot_rows = out_cotangent.astype(jnp.float32)
    gain_grad, shift_grad, bias_grad = lax.psum(
        (jnp.sum(row_grad * normed, axis=0), jnp.sum(row_grad, axis=0), jnp.sum(cot_rows, axis=0)),
        ("fsdp", "tp"),
    )
    qkv_bias_grad, up_bias_grad = lax.psum((qkv_bias_part, up_bias_part), "fsdp")
    scaled = row_grad * norm_gain
    input_grad = (
        cot_rows
        + inverse
        * (
            scaled
            - jnp.mean(scaled, axis=-1, keepdims=True)
            - normed * jnp.mean(scaled * normed, axis=-1, keepdims=True)
        )
    ).astype(jnp.bfloat16)
    return (
        layer_output,
        input_grad,
        gain_grad,
        shift_grad,
        qkv_grad,
        qkv_bias_grad,
        out_grad,
        bias_grad,
        up_grad,
        up_bias_grad,
        down_grad,
        bias_grad,
    )


def solution(mesh):
    in_specs = (
        P(("fsdp", "tp"), None),
        P(("fsdp", "tp"), None),
        P("fsdp", None),
        P(),
        P(),
        P("fsdp", "tp"),
        P("tp"),
        P("tp", "fsdp"),
        P(),
        P("fsdp", "tp"),
        P("tp"),
        P("tp", "fsdp"),
        P(),
    )
    out_specs = (
        P(("fsdp", "tp"), None),
        P(("fsdp", "tp"), None),
        P(),
        P(),
        P("fsdp", "tp"),
        P("tp"),
        P("tp", "fsdp"),
        P(),
        P("fsdp", "tp"),
        P("tp"),
        P("tp", "fsdp"),
        P(),
    )
    return jax.shard_map(body, mesh=mesh, in_specs=in_specs, out_specs=out_specs, check_vma=False)
```

profile of v0, /device:TPU:0, one launch (start us, length us, event | category | flops | bytes accessed | tf_op | source)
XLA Modules:
  0.0 530.0 jit_solution(7264286757015813341)
XLA Ops:
  9.7 2.0 fusion.64
  13.9 34.6 %all_gather.19 = bf16[768,576]{1,0:T(8,128)(2,1)S(1)} all-gather(bf16[96,576]{1,0:T(8,128)(2,1)S(1)} %copy-done.11), channel_id=1, replica_groups=mesh['fsdp'=8,'tp'=4] {'fsdp'}, dimensions={0}, use_global_device_ids=true | all-gather | bytes 995328 | tf_op jit(solution)/shard_map/all_gather | solution.py:165
  49.3 31.3 %all_gather.20 = bf16[192,768]{0,1:T(8,128)(2,1)S(1)} all-gather(bf16[192,96]{0,1:T(8,128)(2,1)S(1)} %copy.81), channel_id=1, replica_groups=mesh['fsdp'=8,'tp'=4] {'fsdp'}, dimensions={1}, use_global_device_ids=true | all-gather | bytes 331776 | tf_op jit(solution)/shard_map/all_gather | solution.py:166
  80.9 2.5 convolution_add_fusion.4
  86.6 16.1 %while.28 = (s32[]{:T(128)}, bf16[3,1024,64]{1,2,0:T(8,128)(2,1)}, f32[3,1024,1]{1,2,0:T(1,128)S(1)}, s32[1024]{0:T(1024)S(1)}, bf16[3,1024,64]{2,1,0:T(8,128)(2...) while((s32[]{:T(128)}, bf16[3,1024,64]{1,2,0:T(8,128)(2,1)}, ...), condition=%wide.region_9.10_spmd, body=%wide.region_4.9_spmd.sunk | while | flops 209518592 | bytes 10947209 | solution.py:183
  88.2 1.8 fusion.151
  102.7 2.1 convolution_convert_fusion.2
  106.0 45.1 %while.29 = (s32[]{:T(128)}, f32[3,1024,64]{1,2,0:T(8,128)}, f32[3,1024,64]{1,2,0:T(8,128)}, f32[3,1024,64]{1,2,0:T(8,128)}, s32[1024]{0:T(1024)S(1)}, /*index=5...) while((s32[]{:T(128)}, f32[3,1024,64]{1,2,0:T(8,128)}, ...), condition=%wide.region_13.14_spmd, body=%wide.region_11.13_spmd.sunk | while | flops 512424960 | bytes 20644056 | solution.py:220
  106.0 1.8 subtract_exponential_fusion.2
  114.4 2.0 fusion.172
  121.0 1.8 subtract_exponential_fusion.2
  129.5 2.0 fusion.172
  136.1 1.8 subtract_exponential_fusion.2
  144.5 2.0 fusion.172
  158.2 2.6 convolution_bitcast_fusion
  161.1 5.4 %multiply_convert_fusion.1 = (bf16[1024,768]{1,0:T(8,128)(2,1)}, f32[1024,768]{1,0:T(8,128)}) fusion(f32[768]{0:T(1024)S(1)} %copy-done.19, bf16[1024,768]{1,0:T(8,128)(2,1)} %all-gather.5.cloned.1.call-done, bf16[768,768]{1,0:T(8,128)(2,1)} %all-gather.7.cloned.1.call-done), kind=kOutput, calls=%fused_computation.93 | convolution fusion | flops 1212678144 | bytes 7474176 | tf_op jit(solution)/shard_map/dot_general | solution.py:185
  166.5 4.1 fusion.91
  172.8 3.1 convolution_add_fusion.2
  176.0 3.2 fusion.92
  179.3 3.3 convolution_add_fusion.3
  182.7 4.5 fusion.93
  187.2 4.8 fusion.74
  192.1 4.3 fusion.94
  197.9 22.1 %all-reduce.3 = (f32[576]{0:T(1024)}, f32[768]{0:T(1024)}) all-reduce(f32[576]{0:T(1024)S(1)} %reduce_sum.120, f32[768]{0:T(1024)S(1)} %get-tuple-element.415), channel_id=1, replica_groups=mesh['fsdp'=8,'tp'=4] {'fsdp'}, use_global_device_ids=true, to_apply=%region_23.24 | all-reduce | flops 1344 | bytes 10752 | tf_op jit(solution)/shard_map/psum | solution.py:245
  220.1 5.1 reduce-scatter.19.cloned.1.call-done
  226.8 37.7 %reduce-scatter.11.cloned.1.call-done = f32[256,768]{1,0:T(8,128)} async-done(((f32[1024,768]{1,0:T(8,128)}), f32[256,768]{1,0:T(8,128)}) %reduce-scatter.11.cloned.1.call-update) | async-done | bytes 786448 | tf_op jit(solution)/shard_map/reduce_scatter | solution.py:239
  266.0 38.9 %reduce-scatter.9.cloned.1.call-done = f32[256,768]{1,0:T(8,128)} async-done(((f32[1024,768]{1,0:T(8,128)}), f32[256,768]{1,0:T(8,128)}) %reduce-scatter.9.cloned.1.call-update) | async-done | bytes 786448 | tf_op jit(solution)/shard_map/reduce_scatter | solution.py:190
  304.9 2.6 convert_reduce_fusion.1
  307.6 40.2 %all-reduce.2 = (f32[768]{0:T(1024)}, f32[768]{0:T(1024)}, f32[768]{0:T(1024)S(1)}) all-reduce(f32[768]{0:T(1024)S(1)} %get-tuple-element.331, f32[768]{0:T(1024)S(1)} %get-tuple-element.334, f32[768]{0:T(1024)S(1)} %get-tuple-element.398), channel_id=1, replica_groups=mesh['fsdp'=8,'tp'=4] {'fsdp','tp'}, use_global_device_ids=true, to_apply=%region_18.19 | all-reduce | flops 2304 | bytes 18432 | tf_op jit(solution)/shard_map/psum | solution.py:241
  347.8 28.9 %reduce-scatter.13.cloned.1.call-done = f32[96,576]{1,0:T(8,128)} async-done(((f32[768,576]{1,0:T(8,128)}), f32[96,576]{1,0:T(8,128)}) %reduce-scatter.13.cloned.1.call-update) | async-done | bytes 221200 | tf_op jit(solution)/shard_map/reduce_scatter | solution.py:234
  376.7 73.0 %reduce-scatter.15.cloned.1.call-done = f32[96,768]{1,0:T(8,128)} async-done(((f32[768,768]{1,0:T(8,128)}), f32[96,768]{1,0:T(8,128)}) %reduce-scatter.15.cloned.1.call-update) | async-done | bytes 294928 | tf_op jit(solution)/shard_map/reduce_scatter | solution.py:236
  449.7 72.9 %reduce-scatter.17.cloned.1.call-done = f32[768,96]{0,1:T(8,128)} async-done(((f32[768,768]{0,1:T(8,128)}), f32[768,96]{0,1:T(8,128)}) %reduce-scatter.17.cloned.1.call-update) | async-done | bytes 294928 | tf_op jit(solution)/shard_map/reduce_scatter | solution.py:237
  (210 shorter events, 72.5 us)
Async XLA Ops:
  7.2 6.7 %copy-start.11 = (bf16[96,576]{1,0:T(8,128)(2,1)S(1)}, bf16[96,576]{1,0:T(8,128)(2,1)}, u32[]{:S(2)}) copy-start(bf16[96,576]{1,0:T(8,128)(2,1)} %param.22) | copy-start | bytes 331780
  7.2 41.3 %copy-start.10 = (s32[1,1024]{1,0:T(1,128)S(1)}, s32[1,1024]{1,0:T(1,128)}, u32[]{:S(2)}) copy-start(s32[1,1024]{1,0:T(1,128)} %param.19) | copy-start | bytes 12292
  7.2 42.0 %copy-start.12 = (bf16[192,96]{1,0:T(8,128)(2,1)S(1)}, bf16[192,96]{1,0:T(8,128)(2,1)}, u32[]{:S(2)}) copy-start(bf16[192,96]{1,0:T(8,128)(2,1)} %param.24) | copy-start | bytes 110596
  7.2 73.7 %all-gather.5.cloned.1.call-start = ((), (), s32[]{:S(2)}) async-start(), calls=%async_computation.6 | async-start | bytes 1966080 | tf_op jit(solution)/shard_map/all_gather | solution.py:162
  8.4 72.5 %copy-start.18 = (f32[576]{0:T(1024)S(1)}, f32[576]{0:T(1024)}, u32[]{:S(2)}) copy-start(f32[576]{0:T(1024)} %param.23) | copy-start | bytes 6916
  11.7 91.0 %all-gather.11.cloned.1.call-start = ((), (), s32[]{:S(2)}) async-start(), calls=%async_computation.10 | async-start | bytes 1966080 | tf_op jit(solution)/shard_map/all_gather | solution.py:192
  12.5 148.6 %all-gather.7.cloned.1.call-start = ((), (), s32[]{:S(2)}) async-start(), calls=%async_computation.7 | async-start | bytes 1327104 | tf_op jit(solution)/shard_map/all_gather | solution.py:167
  13.2 153.3 %all-gather.9.cloned.1.call-start = ((), (), s32[]{:S(2)}) async-start(), calls=%async_computation.8 | async-start | bytes 1327104 | tf_op jit(solution)/shard_map/all_gather | solution.py:168
  13.8 211.3 %reduce-scatter.19.cloned.1.call-start = ((), (), s32[]{:S(2)}) async-start(), calls=%async_computation.15 | async-start | bytes 884736
  48.5 35.0 %copy-start.4 = (bf16[768,576]{1,0:T(8,128)(2,1)}, bf16[768,576]{1,0:T(8,128)(2,1)S(1)}, u32[]{:S(2)}) copy-start(bf16[768,576]{1,0:T(8,128)(2,1)S(1)} %all_gather.19) | copy-start | bytes 2654212
  80.6 22.1 %copy-start.6 = (bf16[192,768]{0,1:T(8,128)(2,1)}, bf16[192,768]{0,1:T(8,128)(2,1)S(1)}, u32[]{:S(2)}) copy-start(bf16[192,768]{0,1:T(8,128)(2,1)S(1)} %all_gather.20) | copy-start | bytes 884740
  110.1 2.8 copy-start
  125.1 2.8 copy-start
  140.2 2.8 copy-start
  151.1 2.3 copy-start.9
  155.5 2.6 copy-start.2
  158.2 2.9 copy-start.19
  160.8 103.7 %reduce-scatter.11.cloned.1.call-start = ((), (), s32[]{:S(2)}) async-start(), calls=%async_computation.11 | async-start | bytes 3932160 | tf_op jit(solution)/shard_map/reduce_scatter | solution.py:239
  166.5 4.2 copy-start.17
  170.7 1.8 copy-start.3
  170.7 2.1 copy-start.5
  175.9 129.0 %reduce-scatter.9.cloned.1.call-start = ((), (), s32[]{:S(2)}) async-start(), calls=%async_computation.9 | async-start | bytes 3932160 | tf_op jit(solution)/shard_map/reduce_scatter | solution.py:190
  176.0 3.2 copy-start.7
  182.6 194.1 %reduce-scatter.13.cloned.1.call-start = ((), (), s32[]{:S(2)}) async-start(), calls=%async_computation.12 | async-start | bytes 2211840 | tf_op jit(solution)/shard_map/reduce_scatter | solution.py:234
  187.2 262.5 %reduce-scatter.15.cloned.1.call-start = ((), (), s32[]{:S(2)}) async-start(), calls=%async_computation.13 | async-start | bytes 2654208 | tf_op jit(solution)/shard_map/reduce_scatter | solution.py:236
  192.0 330.5 %reduce-scatter.17.cloned.1.call-start = ((), (), s32[]{:S(2)}) async-start(), calls=%async_computation.14 | async-start | bytes 2654208 | tf_op jit(solution)/shard_map/reduce_scatter | solution.py:237
  196.4 68.1 %copy-start.1 = (bf16[256,768]{1,0:T(8,128)(2,1)S(1)}, bf16[256,768]{1,0:T(8,128)(2,1)}, u32[]{:S(2)}) copy-start(bf16[256,768]{1,0:T(8,128)(2,1)} %param.17) | copy-start | bytes 1179652
  196.4 68.1 %copy-start.13 = (f32[768]{0:T(1024)S(1)}, f32[768]{0:T(1024)}, u32[]{:S(2)}) copy-start(f32[768]{0:T(1024)} %param.20) | copy-start | bytes 9220
  196.4 108.5 %copy-start.8 = (bf16[256,768]{1,0:T(8,128)(2,1)S(1)}, bf16[256,768]{1,0:T(8,128)(2,1)}, u32[]{:S(2)}) copy-start(bf16[256,768]{1,0:T(8,128)(2,1)} %param.18) | copy-start | bytes 1179652
  196.4 108.5 %copy-start.14 = (f32[768]{0:T(1024)S(1)}, f32[768]{0:T(1024)}, u32[]{:S(2)}) copy-start(f32[768]{0:T(1024)} %param.29) | copy-start | bytes 9220
  196.5 108.5 %copy-start.15 = (f32[768]{0:T(1024)S(1)}, f32[768]{0:T(1024)}, u32[]{:S(2)}) copy-start(f32[768]{0:T(1024)} %param.25) | copy-start | bytes 9220
  347.8 175.4 %copy-start.16 = (f32[768]{0:T(1024)}, f32[768]{0:T(1024)S(1)}, u32[]{:S(2)}) copy-start(f32[768]{0:T(1024)S(1)} %get-tuple-element.670) | copy-start | bytes 9220
  (1 other events, 1.5 us)
Sparse Core Ops, SparseCore 0:
  11.8 22.3 all-gather.4
  35.8 19.6 all-gather.10
  57.7 41.2 all-gather.6
  101.0 40.0 all-gather.8
  160.9 64.1 reduce-scatter.18
  227.5 36.8 reduce-scatter.10
  267.0 37.8 reduce-scatter.8
  309.0 67.6 reduce-scatter.12
  380.8 68.8 reduce-scatter.14
  453.6 68.9 reduce-scatter.16
where the time goes:
time: 531 us; the launch traced here: 530 us
  waiting for transfers between devices  258 us (49%)
  blocking collectives  128 us (24%)
  matrix products  89.1 us (17%)
  other arithmetic  24.5 us (5%)
  between operations  14.6 us (3%)
  local copies, waits for them, and re-layouts  14.2 us (3%)
    reduce_scatter x1, waiting for transfers between devices, body(): lax.psum_scatter(up_grad, 'fsdp', scatter_dimension=0, tiled=True)  73 us
    reduce_scatter x1, waiting for transfers between devices, body(): lax.psum_scatter(down_grad, 'fsdp', scatter_dimension=1, tiled=True)  72.9 us
    psum x1, blocking collectives, body(): lax.psum((jnp.sum(row_grad * normed, axis=0), jnp.sum(row_grad, axis=0),...  40.2 us
    reduce_scatter x1, waiting for transfers between devices, body(): lax.psum_scatter(partial_value, 'tp', scatter_dimension=0, tiled=True)  38.9 us
    reduce_scatter x1, waiting for transfers between devices, body(): lax.psum_scatter(feature_grad, 'tp', scatter_dimension=0, tiled=True)  37.7 us
    dot_general x22, matrix products, cross_cols(): lax.dot_general(left, right, (((1,), (1,)), ((), ())), preferred_element_...  34.8 us
    all_gather x1, blocking collectives, body(): lax.all_gather(qkv_weight, 'fsdp', axis=0, tiled=True)  34.6 us
    all_gather x1, blocking collectives, body(): lax.all_gather(out_weight, 'fsdp', axis=1, tiled=True)  31.3 us
  transfers between devices with their start and end apart: 10, of which 6 were waited for; matrix products, arithmetic and copies ran while one was open for 23% of the time, Pallas kernels for 0%

commit v1 on v0

--- a/solution.py
+++ b/solution.py
@@ -7,6 +7,18 @@
 ROT = 16
 EPSILON = 1e-05
 ROTARY_BASE = 10000.0
+
+
+def doubled_up(x, axis, dim):
+    ways, here, step = (lax.axis_size(axis), lax.axis_index(axis), x.shape[dim])
+    line, have = (x, 1)
+    while have < ways:
+        line = jnp.concatenate(
+            [line, lax.ppermute(line, axis, [(d, (d - have) % ways) for d in range(ways)])],
+            axis=dim,
+        )
+        have = 2 * have
+    return jnp.roll(line, here * step, axis=dim)
 
 
 def layer_norm(values, gain, shift):
@@ -163,7 +175,7 @@
     length = features.shape[0]
     full_qkv, full_out, full_up, full_down = (
         lax.all_gather(qkv_weight, "fsdp", axis=0, tiled=True),
-        lax.all_gather(out_weight, "fsdp", axis=1, tiled=True),
+        doubled_up(out_weight, "fsdp", 1),
         lax.all_gather(up_weight, "fsdp", axis=0, tiled=True),
         lax.all_gather(down_weight, "fsdp", axis=1, tiled=True),
     )

time: 531 us -> 514 us (0.968)
  blocking collectives: 128 us -> 91.5 us
  waiting for transfers between devices: 258 us -> 270 us
  starting transfers between devices: 0.58 us -> 7.36 us
    all_gather x1 -> x0, blocking collectives: 31.3 us -> none  [body(): lax.all_gather(out_weight, 'fsdp', axis=1, tiled=True)]
    ppermute x0 -> x3, waiting for transfers between devices: none -> 11.6 us  [doubled_up(): lax.ppermute(line, axis, [(d, (d - have) % ways) for d in range(ways)])]
    ppermute x0 -> x3, starting transfers between devices: none -> 6.77 us  [doubled_up(): lax.ppermute(line, axis, [(d, (d - have) % ways) for d in range(ways)])]
  transfers between devices with their start and end apart: 10 -> 13, of which waited for: 6 -> 8; matrix products, arithmetic and copies ran while one was open for 23% -> 24% of each run, Pallas kernels for 0% -> 0%
where the time goes in v1:
time: 514 us; the launch traced here: 513 us
  waiting for transfers between devices  270 us (53%)
  blocking collectives  91.5 us (18%)
  matrix products  89.4 us (17%)
  other arithmetic  24.7 us (5%)
  between operations  14.7 us (3%)
  local copies, waits for them, and re-layouts  14.5 us (3%)
  starting transfers between devices  7.36 us (1%)
    reduce_scatter x1, waiting for transfers between devices, body(): lax.psum_scatter(down_grad, 'fsdp', scatter_dimension=1, tiled=True)  72.8 us
    reduce_scatter x1, waiting for transfers between devices, body(): lax.psum_scatter(up_grad, 'fsdp', scatter_dimension=0, tiled=True)  72.8 us
    psum x1, blocking collectives, body(): lax.psum((jnp.sum(row_grad * normed, axis=0), jnp.sum(row_grad, axis=0),...  40.2 us
    reduce_scatter x1, waiting for transfers between devices, body(): lax.psum_scatter(partial_value, 'tp', scatter_dimension=0, tiled=True)  38.9 us
    reduce_scatter x1, waiting for transfers between devices, body(): lax.psum_scatter(feature_grad, 'tp', scatter_dimension=0, tiled=True)  37.6 us
    dot_general x22, matrix products, cross_cols(): lax.dot_general(left, right, (((1,), (1,)), ((), ())), preferred_element_...  34.8 us
    all_gather x1, blocking collectives, body(): lax.all_gather(qkv_weight, 'fsdp', axis=0, tiled=True)  32.7 us
    reduce_scatter x1, waiting for transfers between devices, body(): lax.psum_scatter(qkv_grad, 'fsdp', scatter_dimension=0, tiled=True)  28.9 us
  transfers between devices with their start and end apart: 13, of which 8 were waited for; matrix products, arithmetic and copies ran while one was open for 24% of the time, Pallas kernels for 0%

profile of v1, /device:TPU:0, one launch (start us, length us, event | category | flops | bytes accessed | tf_op | source)
XLA Modules:
  0.0 512.5 jit_solution(12695177688361902886)
XLA Ops:
  9.7 2.0 fusion.64
  13.3 6.1 %collective-permute-start = (bf16[192,96]{1,0:T(8,128)(2,1)S(1)}, bf16[192,96]{1,0:T(8,128)(2,1)S(1)}, u32[]{:S(2)}, u32[]{:S(2)}) collective-permute-start(bf16[192,96]{1,0:T(8,128)(2,1)S(1)} %copy-done.10), channel_id=1, source_target_pairs={{0,28},{4,0},{8,4},{12,8},{16,12},{20,16},{24,20},{28,24},{1,29},{... | collective-permute-start | bytes 110600 | tf_op jit(solution)/shard_map/ppermute | solution.py:17
  19.4 32.7 %all_gather.16 = bf16[768,576]{1,0:T(8,128)(2,1)S(1)} all-gather(bf16[96,576]{1,0:T(8,128)(2,1)S(1)} %copy-done.12), channel_id=1, replica_groups=mesh['fsdp'=8,'tp'=4] {'fsdp'}, dimensions={0}, use_global_device_ids=true | all-gather | bytes 995328 | tf_op jit(solution)/shard_map/all_gather | solution.py:177
  53.6 5.1 collective-permute-done.1
  59.2 6.5 %collective-permute-done.2 = bf16[192,384]{1,0:T(8,128)(2,1)S(1)} collective-permute-done((bf16[192,384]{1,0:T(8,128)(2,1)S(1)}, bf16[192,384]{1,0:T(8,128)(2,1)S(1)}, u32[]{:S(2)}, u32[]{:S(2)}) %collective-permute-start.2) | collective-permute-done | bytes 147488 | tf_op jit(solution)/shard_map/ppermute | solution.py:17
  66.1 2.7 convolution_add_fusion.4
  72.0 16.1 %while.28 = (s32[]{:T(128)}, bf16[3,1024,64]{1,2,0:T(8,128)(2,1)}, f32[3,1024,1]{1,2,0:T(1,128)S(1)}, s32[1024]{0:T(1024)S(1)}, bf16[3,1024,64]{2,1,0:T(8,128)(2...) while((s32[]{:T(128)}, bf16[3,1024,64]{1,2,0:T(8,128)(2,1)}, ...), condition=%wide.region_9.10_spmd, body=%wide.region_4.9_spmd.sunk | while | flops 209518592 | bytes 10947209 | solution.py:195
  88.1 2.1 convolution_convert_fusion.2
  91.4 45.1 %while.29 = (s32[]{:T(128)}, f32[3,1024,64]{1,2,0:T(8,128)}, f32[3,1024,64]{1,2,0:T(8,128)}, f32[3,1024,64]{1,2,0:T(8,128)}, s32[1024]{0:T(1024)S(1)}, /*index=5...) while((s32[]{:T(128)}, f32[3,1024,64]{1,2,0:T(8,128)}, ...), condition=%wide.region_13.14_spmd, body=%wide.region_11.13_spmd.sunk | while | flops 512424960 | bytes 20644056 | solution.py:232
  99.8 2.0 fusion.174
  106.4 1.8 subtract_exponential_fusion.2
  114.8 2.0 fusion.174
  121.4 1.8 subtract_exponential_fusion.2
  129.9 2.0 fusion.174
  143.5 2.6 convolution_bitcast_fusion
  146.5 5.5 %multiply_convert_fusion.1 = (bf16[1024,768]{1,0:T(8,128)(2,1)}, f32[1024,768]{1,0:T(8,128)}) fusion(f32[768]{0:T(1024)S(1)} %copy-done.19, bf16[1024,768]{1,0:T(8,128)(2,1)} %all-gather.5.cloned.1.call-done, bf16[768,768]{1,0:T(8,128)(2,1)} %all-gather.7.cloned.1.call-done), kind=kOutput, calls=%fused_computation.93 | convolution fusion | flops 1212678144 | bytes 7474176 | tf_op jit(solution)/shard_map/dot_general | solution.py:197
  151.9 4.1 fusion.95
  158.2 3.1 convolution_add_fusion.2
  161.4 3.2 fusion.96
  164.7 3.5 convolution_add_fusion.3
  168.2 4.5 fusion.97
  172.8 4.8 fusion.74
  177.6 4.3 fusion.98
  183.5 18.7 %all-reduce.3 = (f32[576]{0:T(1024)}, f32[768]{0:T(1024)}) all-reduce(f32[576]{0:T(1024)S(1)} %reduce_sum.120, f32[768]{0:T(1024)S(1)} %get-tuple-element.415), channel_id=1, replica_groups=mesh['fsdp'=8,'tp'=4] {'fsdp'}, use_global_device_ids=true, to_apply=%region_23.24 | all-reduce | flops 1344 | bytes 10752 | tf_op jit(solution)/shard_map/psum | solution.py:257
  202.1 5.9 %reduce-scatter.19.cloned.1.call-done = f32[96,192]{1,0:T(8,128)} async-done(((f32[768,192]{1,0:T(8,128)}), f32[96,192]{1,0:T(8,128)}) %reduce-scatter.19.cloned.1.call-update) | async-done | bytes 73744
  209.7 37.6 %reduce-scatter.11.cloned.1.call-done = f32[256,768]{1,0:T(8,128)} async-done(((f32[1024,768]{1,0:T(8,128)}), f32[256,768]{1,0:T(8,128)}) %reduce-scatter.11.cloned.1.call-update) | async-done | bytes 786448 | tf_op jit(solution)/shard_map/reduce_scatter | solution.py:251
  248.9 38.9 %reduce-scatter.9.cloned.1.call-done = f32[256,768]{1,0:T(8,128)} async-done(((f32[1024,768]{1,0:T(8,128)}), f32[256,768]{1,0:T(8,128)}) %reduce-scatter.9.cloned.1.call-update) | async-done | bytes 786448 | tf_op jit(solution)/shard_map/reduce_scatter | solution.py:202
  287.8 2.6 convert_reduce_fusion.1
  290.5 40.2 %all-reduce.2 = (f32[768]{0:T(1024)}, f32[768]{0:T(1024)}, f32[768]{0:T(1024)S(1)}) all-reduce(f32[768]{0:T(1024)S(1)} %get-tuple-element.331, f32[768]{0:T(1024)S(1)} %get-tuple-element.334, f32[768]{0:T(1024)S(1)} %get-tuple-element.398), channel_id=1, replica_groups=mesh['fsdp'=8,'tp'=4] {'fsdp','tp'}, use_global_device_ids=true, to_apply=%region_18.19 | all-reduce | flops 2304 | bytes 18432 | tf_op jit(solution)/shard_map/psum | solution.py:253
  330.6 28.9 %reduce-scatter.13.cloned.1.call-done = f32[96,576]{1,0:T(8,128)} async-done(((f32[768,576]{1,0:T(8,128)}), f32[96,576]{1,0:T(8,128)}) %reduce-scatter.13.cloned.1.call-update) | async-done | bytes 221200 | tf_op jit(solution)/shard_map/reduce_scatter | solution.py:246
  359.5 72.8 %reduce-scatter.15.cloned.1.call-done = f32[96,768]{1,0:T(8,128)} async-done(((f32[768,768]{1,0:T(8,128)}), f32[96,768]{1,0:T(8,128)}) %reduce-scatter.15.cloned.1.call-update) | async-done | bytes 294928 | tf_op jit(solution)/shard_map/reduce_scatter | solution.py:248
  432.3 72.8 %reduce-scatter.17.cloned.1.call-done = f32[768,96]{0,1:T(8,128)} async-done(((f32[768,768]{0,1:T(8,128)}), f32[768,96]{0,1:T(8,128)}) %reduce-scatter.17.cloned.1.call-update) | async-done | bytes 294928 | tf_op jit(solution)/shard_map/reduce_scatter | solution.py:249
  (217 shorter events, 76.8 us)
Async XLA Ops:
  7.2 6.1 %copy-start.10 = (bf16[192,96]{1,0:T(8,128)(2,1)S(1)}, bf16[192,96]{1,0:T(8,128)(2,1)}, u32[]{:S(2)}) copy-start(bf16[192,96]{1,0:T(8,128)(2,1)} %param.24) | copy-start | bytes 110596
  7.2 12.2 %copy-start.12 = (bf16[96,576]{1,0:T(8,128)(2,1)S(1)}, bf16[96,576]{1,0:T(8,128)(2,1)}, u32[]{:S(2)}) copy-start(bf16[96,576]{1,0:T(8,128)(2,1)} %param.22) | copy-start | bytes 331780
  7.2 44.9 %copy-start.11 = (s32[1,1024]{1,0:T(1,128)S(1)}, s32[1,1024]{1,0:T(1,128)}, u32[]{:S(2)}) copy-start(s32[1,1024]{1,0:T(1,128)} %param.19) | copy-start | bytes 12292
  7.2 58.9 %all-gather.5.cloned.1.call-start = ((), (), s32[]{:S(2)}) async-start(), calls=%async_computation.6 | async-start | bytes 1966080 | tf_op jit(solution)/shard_map/all_gather | solution.py:174
  11.7 54.4 %copy-start.18 = (f32[576]{0:T(1024)S(1)}, f32[576]{0:T(1024)}, u32[]{:S(2)}) copy-start(f32[576]{0:T(1024)} %param.23) | copy-start | bytes 6916
  11.7 76.4 %all-gather.11.cloned.1.call-start = ((), (), s32[]{:S(2)}) async-start(), calls=%async_computation.10 | async-start | bytes 1966080 | tf_op jit(solution)/shard_map/all_gather | solution.py:204
  12.5 134.0 %all-gather.7.cloned.1.call-start = ((), (), s32[]{:S(2)}) async-start(), calls=%async_computation.7 | async-start | bytes 1327104 | tf_op jit(solution)/shard_map/all_gather | solution.py:179
  13.2 138.7 %all-gather.9.cloned.1.call-start = ((), (), s32[]{:S(2)}) async-start(), calls=%async_computation.8 | async-start | bytes 1327104 | tf_op jit(solution)/shard_map/all_gather | solution.py:180
  13.3 39.6 %collective-permute-start = (bf16[192,96]{1,0:T(8,128)(2,1)S(1)}, bf16[192,96]{1,0:T(8,128)(2,1)S(1)}, u32[]{:S(2)}, u32[]{:S(2)}) collective-permute-start(bf16[192,96]{1,0:T(8,128)(2,1)S(1)} %copy-done.10), channel_id=1, source_target_pairs={{0,28},{4,0},{8,4},{12,8},{16,12},{20,16},{24,20},{28,24},{1,29},{... | collective-permute-start | bytes 110600 | tf_op jit(solution)/shard_map/ppermute | solution.py:17
  19.4 188.7 %reduce-scatter.19.cloned.1.call-start = ((), (), s32[]{:S(2)}) async-start(), calls=%async_computation.15 | async-start | bytes 884736
  52.1 16.7 %copy-start.4 = (bf16[768,576]{1,0:T(8,128)(2,1)}, bf16[768,576]{1,0:T(8,128)(2,1)S(1)}, u32[]{:S(2)}) copy-start(bf16[768,576]{1,0:T(8,128)(2,1)S(1)} %all_gather.16) | copy-start | bytes 2654212
  53.0 5.7 %collective-permute-start.1 = (bf16[192,192]{1,0:T(8,128)(2,1)S(1)}, bf16[192,192]{1,0:T(8,128)(2,1)S(1)}, u32[]{:S(2)}, u32[]{:S(2)}) collective-permute-start(bf16[192,192]{1,0:T(8,128)(2,1)S(1)} %pad_maximum_fusion.2), channel_id=1, source_target_pairs={{0,24},{4,28},{8,0},{12,4},{16,8},{20,12},{24,16},{28,20},{1,25},{... | collective-permute-start | bytes 221192 | tf_op jit(solution)/shard_map/ppermute | solution.py:17
  58.8 6.9 %collective-permute-start.2 = (bf16[192,384]{1,0:T(8,128)(2,1)S(1)}, bf16[192,384]{1,0:T(8,128)(2,1)S(1)}, u32[]{:S(2)}, u32[]{:S(2)}) collective-permute-start(bf16[192,384]{1,0:T(8,128)(2,1)S(1)} %pad_maximum_fusion.1), channel_id=1, source_target_pairs={{0,16},{4,20},{8,24},{12,28},{16,0},{20,4},{24,8},{28,12},{1,17},{... | collective-permute-start | bytes 442376 | tf_op jit(solution)/shard_map/ppermute | solution.py:17
  66.1 22.1 %copy-start.6 = (bf16[192,1536]{1,0:T(8,128)(2,1)}, bf16[192,1536]{1,0:T(8,128)(2,1)S(1)}, u32[]{:S(2)}) copy-start(bf16[192,1536]{1,0:T(8,128)(2,1)S(1)} %concatenate.73) | copy-start | bytes 1769476
  95.5 2.8 copy-start
  110.5 2.8 copy-start
  125.6 2.8 copy-start
  140.9 2.6 copy-start.2
  143.5 2.9 copy-start.19
  146.2 101.2 %reduce-scatter.11.cloned.1.call-start = ((), (), s32[]{:S(2)}) async-start(), calls=%async_computation.11 | async-start | bytes 3932160 | tf_op jit(solution)/shard_map/reduce_scatter | solution.py:251
  151.9 4.2 copy-start.17
  161.4 126.4 %reduce-scatter.9.cloned.1.call-start = ((), (), s32[]{:S(2)}) async-start(), calls=%async_computation.9 | async-start | bytes 3932160 | tf_op jit(solution)/shard_map/reduce_scatter | solution.py:202
  161.4 3.2 copy-start.7
  168.2 191.4 %reduce-scatter.13.cloned.1.call-start = ((), (), s32[]{:S(2)}) async-start(), calls=%async_computation.12 | async-start | bytes 2211840 | tf_op jit(solution)/shard_map/reduce_scatter | solution.py:246
  172.7 259.6 %reduce-scatter.15.cloned.1.call-start = ((), (), s32[]{:S(2)}) async-start(), calls=%async_computation.13 | async-start | bytes 2654208 | tf_op jit(solution)/shard_map/reduce_scatter | solution.py:248
  177.5 327.5 %reduce-scatter.17.cloned.1.call-start = ((), (), s32[]{:S(2)}) async-start(), calls=%async_computation.14 | async-start | bytes 2654208 | tf_op jit(solution)/shard_map/reduce_scatter | solution.py:249
  181.9 65.4 %copy-start.1 = (bf16[256,768]{1,0:T(8,128)(2,1)S(1)}, bf16[256,768]{1,0:T(8,128)(2,1)}, u32[]{:S(2)}) copy-start(bf16[256,768]{1,0:T(8,128)(2,1)} %param.17) | copy-start | bytes 1179652
  181.9 65.4 %copy-start.13 = (f32[768]{0:T(1024)S(1)}, f32[768]{0:T(1024)}, u32[]{:S(2)}) copy-start(f32[768]{0:T(1024)} %param.20) | copy-start | bytes 9220
  182.0 105.9 %copy-start.8 = (bf16[256,768]{1,0:T(8,128)(2,1)S(1)}, bf16[256,768]{1,0:T(8,128)(2,1)}, u32[]{:S(2)}) copy-start(bf16[256,768]{1,0:T(8,128)(2,1)} %param.18) | copy-start | bytes 1179652
  182.0 105.8 %copy-start.14 = (f32[768]{0:T(1024)S(1)}, f32[768]{0:T(1024)}, u32[]{:S(2)}) copy-start(f32[768]{0:T(1024)} %param.29) | copy-start | bytes 9220
  182.0 105.8 %copy-start.15 = (f32[768]{0:T(1024)S(1)}, f32[768]{0:T(1024)}, u32[]{:S(2)}) copy-start(f32[768]{0:T(1024)} %param.25) | copy-start | bytes 9220
  330.6 175.1 %copy-start.16 = (f32[768]{0:T(1024)}, f32[768]{0:T(1024)S(1)}, u32[]{:S(2)}) copy-start(f32[768]{0:T(1024)S(1)} %get-tuple-element.670) | copy-start | bytes 9220
  (4 other events, 7.7 us)
Sparse Core Ops, SparseCore 0:
  11.8 22.3 all-gather.4
  35.8 19.6 all-gather.10
  57.6 41.1 all-gather.6
  100.9 39.8 all-gather.8
  146.3 61.7 reduce-scatter.18
  210.5 36.8 reduce-scatter.10
  249.9 37.8 reduce-scatter.8
  291.9 67.6 reduce-scatter.12
  363.6 68.6 reduce-scatter.14
  436.2 68.8 reduce-scatter.16
